TPU v7x, 32 devices: a whole 2x2x4 slice. The times are simulated.
32 devices in a mesh: shard: 2 (over x), ctx: 4 (over z), tp: 4 (over y, core).
Axes of the slice: x: 2, y: 2, z: 4, core: 2. Of those that a mesh axis runs over, the one named last changes fastest.
Arguments:
- frames: bfloat16 [2, 2, 2048, 1280], P(None, 'shard', 'ctx'), may hold values from -6 to 6
- lengths: int32 [2, 2], P(None, 'shard'), may hold values from 0 to 2048, as said below
- first_gain: bfloat16 [1280], replicated, may hold values from 0.25 to 1.75
- first_bias: bfloat16 [1280], replicated, may hold values from -3 to 3
- query_weight: bfloat16 [1280, 1280], P('shard', 'tp'), may hold values from -0.15625 to 0.15625
- query_bias: bfloat16 [1280], P('tp'), may hold values from -3 to 3
- key_weight: bfloat16 [1280, 1280], P('shard', 'tp'), may hold values from -0.15625 to 0.15625
- value_weight: bfloat16 [1280, 1280], P('shard', 'tp'), may hold values from -0.15625 to 0.15625
- value_bias: bfloat16 [1280], P('tp'), may hold values from -0.088378906 to 0.088378906
- output_weight: bfloat16 [1280, 1280], P('shard', 'tp'), may hold values from -4 to 4
- output_bias: bfloat16 [1280], replicated, may hold values from -3 to 3
- second_gain: bfloat16 [1280], replicated, may hold values from 0.25 to 1.75
- second_bias: bfloat16 [1280], replicated, may hold values from -3 to 3
- inner_weight: bfloat16 [1280, 5120], P('shard', 'tp'), may hold values from -0.15625 to 0.15625
- inner_bias: bfloat16 [5120], P('tp'), may hold values from -3 to 3
- outer_weight: bfloat16 [1280, 5120], P('shard', 'tp'), may hold values from -0.15625 to 0.15625
- outer_bias: bfloat16 [1280], replicated, may hold values from -3 to 3
- cotangent: bfloat16 [2, 2, 2048, 1280], P(None, 'shard', 'ctx'), may hold values from -6 to 6
Outputs:
- result: bfloat16 [2, 2, 2048, 1280], P(None, 'shard', 'ctx')
- frames_grad: bfloat16 [2, 2, 2048, 1280], P(None, 'shard', 'ctx')
- first_gain_grad: float32 [1280], replicated
- first_bias_grad: float32 [1280], replicated
- query_weight_grad: float32 [1280, 1280], P('shard', 'tp')
- query_bias_grad: float32 [1280], P('tp')
- key_weight_grad: float32 [1280, 1280], P('shard', 'tp')
- value_weight_grad: float32 [1280, 1280], P('shard', 'tp')
- value_bias_grad: float32 [1280], P('tp')
- output_weight_grad: float32 [1280, 1280], P('shard', 'tp')
- output_bias_grad: float32 [1280], replicated
- second_gain_grad: float32 [1280], replicated
- second_bias_grad: float32 [1280], replicated
- inner_weight_grad: float32 [1280, 5120], P('shard', 'tp')
- inner_bias_grad: float32 [5120], P('tp')
- outer_weight_grad: float32 [1280, 5120], P('shard', 'tp')
- outer_bias_grad: float32 [1280], replicated
Inputs may be any that keep to these rules, and one draw needn't show every extreme that they name: Slot lengths count a clip's first frames; 0 marks an empty slot; in every draw some slot is empty and some slot is full.
All inputs are finite; a program needn't handle non-finite values.
Results may differ from a plain program's by a relative error of at most 0.025.
Values may be sent and summed in bfloat16 or wider, within the bound.
No kernel may reach another device: no remote copies, remote signals or barrier semaphores. Data moves between devices by JAX's collectives and lax.ppermute only.
A program may use at most 192 MiB of HBM per device.

v0:
```python
import math
import jax
import jax.numpy as jnp
from jax import lax
from jax.sharding import PartitionSpec as P

HD = 80
epsilon = 1e-05


def layer_norm(values, scale_gain, shift_bias):
    center = values - jnp.mean(values, -1, keepdims=True)
    spread = jnp.mean(center * center, -1, keepdims=True)
    return center * lax.rsqrt(spread + epsilon) * scale_gain + shift_bias


def per_device(
    frames,
    lengths,
    first_gain,
    first_bias,
    query_weight,
    query_bias,
    key_weight,
    value_weight,
    value_bias,
    output_weight,
    output_bias,
    second_gain,
    second_bias,
    inner_weight,
    inner_bias,
    outer_weight,
    outer_bias,
    cotangent,
):
    float_kind = jnp.float32
    half_kind = jnp.bfloat16
    batch_count = frames.shape[0]
    frame_rows = frames.shape[2]
    group_width = query_weight.shape[1]
    head_count = group_width // HD
    scaling = 1.0 / math.sqrt(HD)
    slot_frames = frame_rows * lax.axis_size("ctx")
    key_block = min(512, slot_frames)
    positions = lax.axis_index("ctx") * frame_rows + jnp.arange(frame_rows, dtype=jnp.int32)
    gain_one = first_gain.astype(float_kind)
    bias_one = first_bias.astype(float_kind)
    gain_two = second_gain.astype(float_kind)
    bias_two = second_bias.astype(float_kind)
    query_shift = query_bias.astype(float_kind)
    value_shift = value_bias.astype(float_kind)
    output_shift = output_bias.astype(float_kind)
    inner_shift = inner_bias.astype(float_kind)
    outer_shift = outer_bias.astype(float_kind)
    shards = (query_weight, key_weight, value_weight, output_weight, inner_weight, outer_weight)
    contract_last = (((1,), (1,)), ((), ()))
    contract_rows = (((0,), (0,)), ((), ()))
    results = []
    frame_grads = []
    small_totals = None
    weight_totals = None
    for batch_index in range(batch_count):
        gathered = (
            lax.all_gather(shards[0], "shard", axis=0, tiled=True),
            lax.all_gather(shards[1], "shard", axis=0, tiled=True),
            lax.all_gather(shards[2], "shard", axis=0, tiled=True),
            lax.all_gather(shards[3], "shard", axis=0, tiled=True),
            lax.all_gather(shards[4], "shard", axis=0, tiled=True),
            lax.all_gather(shards[5], "shard", axis=0, tiled=True),
        )
        full_query, full_key, full_value, full_output, full_inner, full_outer = gathered
        clip_frames = frames[batch_index, 0].astype(float_kind)
        length = lengths[batch_index, 0]
        frame_valid = positions < length
        has_frames = length > 0
        normed, first_back = jax.vjp(layer_norm, clip_frames, gain_one, bias_one)
        normed_low = normed.astype(half_kind)
        queries = (
            jnp.dot(normed_low, full_query, preferred_element_type=float_kind) + query_shift
        ).astype(half_kind)
        key_rows = jnp.dot(normed_low, full_key, preferred_element_type=float_kind).astype(
            half_kind
        )
        value_rows = (
            jnp.dot(normed_low, full_value, preferred_element_type=float_kind) + value_shift
        ).astype(half_kind)
        query_heads = queries.reshape(frame_rows, head_count, HD)
        start = jnp.int32(0)
        key_piece = lax.all_gather(key_rows, "ctx", axis=0, tiled=True)
        value_piece = lax.all_gather(value_rows, "ctx", axis=0, tiled=True)
        unnormal = jnp.zeros((frame_rows, head_count, HD), float_kind)
        weight_total = jnp.zeros((frame_rows, head_count), float_kind)
        piece_rows = key_piece.shape[0]
        for begin in range(0, piece_rows, key_block):
            count = min(key_block, piece_rows - begin)
            key_part = key_piece[begin : begin + count].reshape(count, head_count, HD)
            value_part = value_piece[begin : begin + count].reshape(count, head_count, HD)
            scores = (
                jnp.einsum("qhd,khd->hqk", query_heads, key_part, preferred_element_type=float_kind)
                * scaling
            )
            key_valid = start + begin + jnp.arange(count, dtype=jnp.int32) < length
            expo = jnp.where(key_valid[None, None, :], jnp.exp(scores), 0.0)
            weight_total = weight_total + jnp.sum(expo, -1).T
            unnormal = unnormal + jnp.einsum(
                "hqk,khd->qhd",
                expo.astype(half_kind),
                value_part,
                preferred_element_type=float_kind,
            )
        unnormal, weight_total = (unnormal, weight_total)
        denominator = jnp.where(has_frames, weight_total, 1.0)
        attended = unnormal / denominator[:, :, None]
        mixed_low = attended.reshape(frame_rows, group_width).astype(half_kind)
        partial_out = lax.dot_general(
            mixed_low, full_output, contract_last, preferred_element_type=float_kind
        )
        middle = (
            clip_frames
            + lax.psum(partial_out.astype(jnp.bfloat16), "tp").astype(jnp.float32)
            + output_shift
        )
        normed_two, second_back = jax.vjp(layer_norm, middle, gain_two, bias_two)
        normed_two_low = normed_two.astype(half_kind)
        inner_linear = (
            jnp.dot(normed_two_low, full_inner, preferred_element_type=float_kind) + inner_shift
        )
        activated, gelu_back = jax.vjp(
            lambda value_in: jax.nn.gelu(value_in, approximate=False), inner_linear
        )
        activated_low = activated.astype(half_kind)
        partial_ffn = lax.dot_general(
            activated_low, full_outer, contract_last, preferred_element_type=float_kind
        )
        final = (
            middle
            + lax.psum(partial_ffn.astype(jnp.bfloat16), "tp").astype(jnp.float32)
            + outer_shift
        )
        results.append(final.astype(half_kind))
        back_weights = (
            lax.all_gather(shards[0], "shard", axis=0, tiled=True),
            lax.all_gather(shards[1], "shard", axis=0, tiled=True),
            lax.all_gather(shards[2], "shard", axis=0, tiled=True),
            lax.all_gather(shards[3], "shard", axis=0, tiled=True),
            lax.all_gather(shards[4], "shard", axis=0, tiled=True),
            lax.all_gather(shards[5], "shard", axis=0, tiled=True),
        )
        back_query, back_key, back_value, back_output, back_inner, back_outer = back_weights
        grad_final = cotangent[batch_index, 0].astype(float_kind) * frame_valid[:, None].astype(
            float_kind
        )
        final_low = grad_final.astype(half_kind)
        grad_outer = lax.dot_general(
            final_low, activated_low, contract_rows, preferred_element_type=float_kind
        )
        grad_activated = jnp.dot(final_low, back_outer, preferred_element_type=float_kind)
        grad_inner = gelu_back(grad_activated)[0]
        inner_low = grad_inner.astype(half_kind)
        grad_inner_weight = lax.dot_general(
            normed_two_low, inner_low, contract_rows, preferred_element_type=float_kind
        )
        partial_two = lax.dot_general(
            inner_low, back_inner, contract_last, preferred_element_type=float_kind
        )
        grad_normed_two = lax.psum(partial_two.astype(jnp.bfloat16), "tp").astype(jnp.float32)
        grad_middle_norm, grad_gain_two, grad_bias_two = second_back(grad_normed_two)
        grad_middle = grad_final + grad_middle_norm
        middle_low = grad_middle.astype(half_kind)
        grad_output_weight = lax.dot_general(
            middle_low, mixed_low, contract_rows, preferred_element_type=float_kind
        )
        grad_attended = jnp.dot(middle_low, back_output, preferred_element_type=float_kind)
        grad_heads = grad_attended.reshape(frame_rows, head_count, HD)
        scaled_grad = (grad_heads / denominator[:, :, None]).astype(half_kind)
        delta_rows = (jnp.sum(grad_heads * attended, -1) / denominator).T
        all_keys, all_values = (
            lax.all_gather(key_rows, "ctx", axis=0, tiled=True),
            lax.all_gather(value_rows, "ctx", axis=0, tiled=True),
        )

        def key_step(grad_query, block_index):
            begin = block_index * key_block
            key_part = lax.dynamic_slice_in_dim(all_keys, begin, key_block, 0).reshape(
                key_block, head_count, HD
            )
            value_part = lax.dynamic_slice_in_dim(all_values, begin, key_block, 0).reshape(
                key_block, head_count, HD
            )
            scores = (
                jnp.einsum("qhd,khd->hqk", query_heads, key_part, preferred_element_type=float_kind)
                * scaling
            )
            key_valid = begin + jnp.arange(key_block, dtype=jnp.int32) < length
            expo = jnp.where(key_valid[None, None, :], jnp.exp(scores), 0.0)
            through_values = jnp.einsum(
                "qhd,khd->hqk", scaled_grad, value_part, preferred_element_type=float_kind
            )
            grad_scores = (scaling * expo * (through_values - delta_rows[:, :, None])).astype(
                half_kind
            )
            grad_query = grad_query + jnp.einsum(
                "hqk,khd->qhd", grad_scores, key_part, preferred_element_type=float_kind
            )
            key_term = jnp.einsum(
                "hqk,qhd->khd", grad_scores, query_heads, preferred_element_type=float_kind
            )
            value_term = jnp.einsum(
                "hqk,qhd->khd",
                expo.astype(half_kind),
                scaled_grad,
                preferred_element_type=float_kind,
            )
            return (grad_query, (key_term, value_term))

        grad_query, (key_terms, value_terms) = lax.scan(
            key_step,
            jnp.zeros((frame_rows, head_count, HD), float_kind),
            jnp.arange(slot_frames // key_block),
        )
        key_terms = key_terms.reshape(slot_frames, group_width)
        value_terms = value_terms.reshape(slot_frames, group_width)
        grad_keys, grad_values = (
            lax.psum_scatter(
                key_terms.astype(jnp.bfloat16), "ctx", scatter_dimension=0, tiled=True
            ).astype(jnp.float32),
            lax.psum_scatter(
                value_terms.astype(jnp.bfloat16), "ctx", scatter_dimension=0, tiled=True
            ).astype(jnp.float32),
        )
        query_low = grad_query.reshape(frame_rows, group_width).astype(half_kind)
        keys_low = grad_keys.astype(half_kind)
        values_low = grad_values.astype(half_kind)
        grad_query_weight = lax.dot_general(
            normed_low, query_low, contract_rows, preferred_element_type=float_kind
        )
        grad_key_weight = lax.dot_general(
            normed_low, keys_low, contract_rows, preferred_element_type=float_kind
        )
        grad_value_weight = lax.dot_general(
            normed_low, values_low, contract_rows, preferred_element_type=float_kind
        )
        partial_one = lax.dot_general(
            query_low, back_query, contract_last, preferred_element_type=float_kind
        )
        partial_one = partial_one + lax.dot_general(
            keys_low, back_key, contract_last, preferred_element_type=float_kind
        )
        partial_one = partial_one + lax.dot_general(
            values_low, back_value, contract_last, preferred_element_type=float_kind
        )
        grad_normed = lax.psum(partial_one.astype(jnp.bfloat16), "tp").astype(jnp.float32)
        grad_frames_norm, grad_gain_one, grad_bias_one = first_back(grad_normed)
        frame_grads.append((grad_middle + grad_frames_norm).astype(half_kind))
        small_terms = (
            grad_gain_one,
            grad_bias_one,
            jnp.sum(query_low.astype(float_kind), 0),
            jnp.sum(values_low.astype(float_kind), 0),
            jnp.sum(grad_middle, 0),
            grad_gain_two,
            grad_bias_two,
            jnp.sum(grad_inner, 0),
            jnp.sum(grad_final, 0),
        )
        small_totals = (
            small_terms
            if small_totals is None
            else jax.tree.map(jnp.add, small_totals, small_terms)
        )
        local_grads = (
            grad_query_weight,
            grad_key_weight,
            grad_value_weight,
            grad_output_weight,
            grad_inner_weight,
            grad_outer,
        )
        scattered = (
            lax.psum_scatter(
                local_grads[0].astype(jnp.bfloat16), "shard", scatter_dimension=0, tiled=True
            ).astype(jnp.float32),
            lax.psum_scatter(
                local_grads[1].astype(jnp.bfloat16), "shard", scatter_dimension=0, tiled=True
            ).astype(jnp.float32),
            lax.psum_scatter(
                local_grads[2].astype(jnp.bfloat16), "shard", scatter_dimension=0, tiled=True
            ).astype(jnp.float32),
            lax.psum_scatter(
                local_grads[3].astype(jnp.bfloat16), "shard", scatter_dimension=0, tiled=True
            ).astype(jnp.float32),
            lax.psum_scatter(
                local_grads[4].astype(jnp.bfloat16), "shard", scatter_dimension=0, tiled=True
            ).astype(jnp.float32),
            lax.psum_scatter(
                local_grads[5].astype(jnp.bfloat16), "shard", scatter_dimension=0, tiled=True
            ).astype(jnp.float32),
        )
        contribution = (
            lax.psum(scattered[0].astype(jnp.bfloat16), "ctx").astype(jnp.float32),
            lax.psum(scattered[1].astype(jnp.bfloat16), "ctx").astype(jnp.float32),
            lax.psum(scattered[2].astype(jnp.bfloat16), "ctx").astype(jnp.float32),
            lax.psum(scattered[3].astype(jnp.bfloat16), "ctx").astype(jnp.float32),
            lax.psum(scattered[4].astype(jnp.bfloat16), "ctx").astype(jnp.float32),
            lax.psum(scattered[5].astype(jnp.bfloat16), "ctx").astype(jnp.float32),
        )
        weight_totals = (
            contribution
            if weight_totals is None
            else jax.tree.map(jnp.add, weight_totals, contribution)
        )
    small_totals = lax.psum(small_totals, ("shard", "ctx"))
    return (
        jnp.stack(results)[:, None],
        jnp.stack(frame_grads)[:, None],
        small_totals[0],
        small_totals[1],
        weight_totals[0],
        small_totals[2],
        weight_totals[1],
        weight_totals[2],
        small_totals[3],
        weight_totals[3],
        small_totals[4],
        small_totals[5],
        small_totals[6],
        weight_totals[4],
        small_totals[7],
        weight_totals[5],
        small_totals[8],
    )


def solution(mesh):
    return jax.shard_map(
        per_device,
        mesh=mesh,
        in_specs=(
            P(None, "shard", "ctx", None),
            P(None, "shard"),
            P(),
            P(),
            P("shard", "tp"),
            P("tp"),
            P("shard", "tp"),
            P("shard", "tp"),
            P("tp"),
            P("shard", "tp"),
            P(),
            P(),
            P(),
            P("shard", "tp"),
            P("tp"),
            P("shard", "tp"),
            P(),
            P(None, "shard", "ctx", None),
        ),
        out_specs=(
            P(None, "shard", "ctx", None),
            P(None, "shard", "ctx", None),
            P(),
            P(),
            P("shard", "tp"),
            P("tp"),
            P("shard", "tp"),
            P("shard", "tp"),
            P("tp"),
            P("shard", "tp"),
            P(),
            P(),
            P(),
            P("shard", "tp"),
            P("tp"),
            P("shard", "tp"),
            P(),
        ),
        check_vma=False,
    )
```

profile of v0, /device:TPU:0, one launch (start us, length us, event | category | flops | bytes accessed | tf_op | source)
XLA Modules:
  0.0 1457.8 jit_solution(4725034005878868603)
XLA Ops:
  11.6 13.1 all_gather.23
  82.5 13.6 all-gather.7.cloned.1.call-done
  109.2 37.8 %all-reduce.10.cloned.1.call-done = bf16[512,1280]{1,0:T(8,128)(2,1)} async-done(((bf16[512,1280]{1,0:T(8,128)(2,1)}), bf16[512,1280]{1,0:T(8,128)(2,1)}) %all-reduce.10.cloned.1.call-update) | async-done | bytes 1310736 | tf_op jit(solution)/shard_map/psum | solution.py:121
  160.3 24.6 %all-gather.17.cloned.1.call-done = bf16[2048,320]{0,1:T(8,128)(2,1)} async-done(((bf16[512,320]{0,1:T(8,128)(2,1)}), bf16[2048,320]{0,1:T(8,128)(2,1)}) %all-gather.17.cloned.1.call-update) | async-done | bytes 1310736 | tf_op jit(solution)/shard_map/all_gather | solution.py:90
  190.2 28.3 %all-gather.15.cloned.1.call-done = bf16[2048,320]{0,1:T(8,128)(2,1)} async-done(((bf16[512,320]{0,1:T(8,128)(2,1)}), bf16[2048,320]{0,1:T(8,128)(2,1)}) %all-gather.15.cloned.1.call-update) | async-done | bytes 1310736 | tf_op jit(solution)/shard_map/all_gather | solution.py:91
  235.4 35.5 %all-reduce.12.cloned.1.call-done = bf16[512,1280]{1,0:T(8,128)(2,1)} async-done(((bf16[512,1280]{1,0:T(8,128)(2,1)}), bf16[512,1280]{1,0:T(8,128)(2,1)}) %all-reduce.12.cloned.1.call-update) | async-done | bytes 1310736 | tf_op jit(solution)/shard_map/psum | solution.py:121
  301.3 26.4 %all-gather.13.cloned.1.call-done = bf16[1280,1280]{1,0:T(8,128)(2,1)} async-done(((bf16[640,1280]{1,0:T(8,128)(2,1)}), bf16[1280,1280]{1,0:T(8,128)(2,1)}) %all-gather.13.cloned.1.call-update) | async-done | bytes 3276816 | tf_op jit(solution)/shard_map/all_gather | solution.py:70
  347.2 60.0 %all-reduce.16.cloned.1.call-done = (bf16[512,1280]{1,0:T(8,128)(2,1)}, bf16[512,1280]{1,0:T(8,128)(2,1)}) async-done(((bf16[512,1280]{1,0:T(8,128)(2,1)}, bf16[512,1280]{1,0:T(8,128)(2,1)}), (bf16[512,1280]{1,0:T(8,128)(2,1)}, bf16[512,1280]{1,0:T(8,128)(2,1)})) %all-reduce.16.cloned.1.call-update) | async-done | bytes 2621456 | tf_op jit(solution)/shard_map/psum | solution.py:167
  423.3 60.1 %while.31 = (s32[]{:T(128)}, f32[512,4,80]{0,2,1:T(8,128)}, bf16[4,512,4,80]{1,3,2,0:T(8,128)(2,1)}, bf16[4,512,4,80]{1,3,2,0:T(8,128)(2,1)}, s32[4]{0:T(128)S(1...) while((s32[]{:T(128)}, f32[512,4,80]{0,2,1:T(8,128)}, ...), condition=%wide.region_36.37_spmd.clone, body=%wide.region_35.36_spmd.clone.sunk | while | flops 848626688 | bytes 52898636 | solution.py:217
  498.5 60.2 %while.30 = (s32[]{:T(128)}, f32[512,4,80]{0,2,1:T(8,128)}, bf16[4,512,4,80]{1,3,2,0:T(8,128)(2,1)}, bf16[4,512,4,80]{1,3,2,0:T(8,128)(2,1)}, s32[4]{0:T(128)S(1...) while((s32[]{:T(128)}, f32[512,4,80]{0,2,1:T(8,128)}, ...), condition=%wide.region_25.26_spmd.clone, body=%wide.region_24.25_spmd.clone.sunk | while | flops 848626688 | bytes 52898636 | solution.py:217
  597.3 29.0 %reduce-scatter.35.cloned.1.call-done = bf16[512,320]{0,1:T(8,128)(2,1)} async-done(((bf16[2048,320]{0,1:T(8,128)(2,1)}), bf16[512,320]{0,1:T(8,128)(2,1)}) %reduce-scatter.35.cloned.1.call-update) | async-done | bytes 327696 | tf_op jit(solution)/shard_map/reduce_scatter | solution.py:228
  673.4 17.1 %reduce-scatter.51.cloned.1.call-done = bf16[640,320]{1,0:T(8,128)(2,1)} async-done(((bf16[1280,320]{1,0:T(8,128)(2,1)}), bf16[640,320]{1,0:T(8,128)(2,1)}) %reduce-scatter.51.cloned.1.call-update) | async-done | bytes 409616
  692.5 19.9 %reduce-scatter.49.cloned.1.call-done = bf16[640,320]{1,0:T(8,128)(2,1)} async-done(((bf16[1280,320]{1,0:T(8,128)(2,1)}), bf16[640,320]{1,0:T(8,128)(2,1)}) %reduce-scatter.49.cloned.1.call-update) | async-done | bytes 409616
  714.3 19.9 %reduce-scatter.55.cloned.1.call-done = bf16[640,320]{1,0:T(8,128)(2,1)} async-done(((bf16[1280,320]{1,0:T(8,128)(2,1)}), bf16[640,320]{1,0:T(8,128)(2,1)}) %reduce-scatter.55.cloned.1.call-update) | async-done | bytes 409616
  736.2 19.9 %reduce-scatter.59.cloned.1.call-done = bf16[640,320]{1,0:T(8,128)(2,1)} async-done(((bf16[1280,320]{1,0:T(8,128)(2,1)}), bf16[640,320]{1,0:T(8,128)(2,1)}) %reduce-scatter.59.cloned.1.call-update) | async-done | bytes 409616
  758.0 19.9 %reduce-scatter.53.cloned.1.call-done = bf16[640,320]{1,0:T(8,128)(2,1)} async-done(((bf16[1280,320]{1,0:T(8,128)(2,1)}), bf16[640,320]{1,0:T(8,128)(2,1)}) %reduce-scatter.53.cloned.1.call-update) | async-done | bytes 409616
  779.8 20.0 %reduce-scatter.57.cloned.1.call-done = bf16[640,320]{1,0:T(8,128)(2,1)} async-done(((bf16[1280,320]{1,0:T(8,128)(2,1)}), bf16[640,320]{1,0:T(8,128)(2,1)}) %reduce-scatter.57.cloned.1.call-update) | async-done | bytes 409616
  801.8 45.6 %reduce-scatter.41.cloned.1.call-done = bf16[640,1280]{1,0:T(8,128)(2,1)} async-done(((bf16[1280,1280]{1,0:T(8,128)(2,1)}), bf16[640,1280]{1,0:T(8,128)(2,1)}) %reduce-scatter.41.cloned.1.call-update) | async-done | bytes 1638416 | tf_op jit(solution)/shard_map/reduce_scatter | solution.py:293
  847.4 47.7 %reduce-scatter.43.cloned.1.call-done = bf16[640,1280]{1,0:T(8,128)(2,1)} async-done(((bf16[1280,1280]{1,0:T(8,128)(2,1)}), bf16[640,1280]{1,0:T(8,128)(2,1)}) %reduce-scatter.43.cloned.1.call-update) | async-done | bytes 1638416 | tf_op jit(solution)/shard_map/reduce_scatter | solution.py:293
  895.1 47.2 %reduce-scatter.45.cloned.1.call-done = bf16[640,1280]{1,0:T(8,128)(2,1)} async-done(((bf16[1280,1280]{1,0:T(8,128)(2,1)}), bf16[640,1280]{1,0:T(8,128)(2,1)}) %reduce-scatter.45.cloned.1.call-update) | async-done | bytes 1638416 | tf_op jit(solution)/shard_map/reduce_scatter | solution.py:296
  942.3 47.2 %reduce-scatter.47.cloned.1.call-done = bf16[640,1280]{1,0:T(8,128)(2,1)} async-done(((bf16[1280,1280]{1,0:T(8,128)(2,1)}), bf16[640,1280]{1,0:T(8,128)(2,1)}) %reduce-scatter.47.cloned.1.call-update) | async-done | bytes 1638416 | tf_op jit(solution)/shard_map/reduce_scatter | solution.py:296
  990.7 103.8 %all-reduce.14.cloned.1.call-done = (bf16[512,1280]{1,0:T(8,128)(2,1)}, bf16[512,1280]{1,0:T(8,128)(2,1)}, bf16[512,1280]{1,0:T(8,128)(2,1)}, bf16[512,1280]{1,0:T(8,128)(2,1)}) async-done(((bf16[512,1280]{1,0:T(8,128)(2,1)}, bf16[512,1280]{1,0:T(8,128)(2,1)}, bf16[512,1280]{1,0:T(8,128)(2,1)}, bf16[512,1280]{1,0:T(8,128)(2,1)}), (bf16[512,1280]{1,0:T(8,128)(2,1)}, bf16[512,1280]{1,0:T(8,128)(2,1)}, ...) | async-done | bytes 5242896 | tf_op jit(solution)/shard_map/psum | solution.py:138
  1104.4 41.7 %all-reduce = (f32[1280]{0:T(1024)}, f32[1280]{0:T(1024)}, f32[320]{0:T(512)}, f32[320]{0:T(512)}, f32[1280]{0:T(1024)}, /*index=5*/f32[1280]{0:T(1024)}, f32[1280]{0:T(1024)}, f32[1280]{0:T(1024)}, f32[1280]{0:T(1024)}) all-reduce(f32[1280]{0:T(1024)S(1)} %add.526, ...), channel_id=1, replica_groups=mesh['shard'=2,'ctx'=4,'tp'=4] {'shard','ctx'}, use_global_device_ids=true, to_apply=%region_44.45 | all-reduce | flops 9600 | bytes 76800 | tf_op jit(solution)/shard_map/psum | solution.py:313
  1154.9 285.4 %all-reduce.18.cloned.1.call-done = (bf16[640,320]{0,1:T(8,128)(2,1)}, bf16[640,320]{0,1:T(8,128)(2,1)}, bf16[640,320]{0,1:T(8,128)(2,1)}, bf16[640,320]{0,1:T(8...) async-done(((bf16[640,320]{0,1:T(8,128)(2,1)}, ...) | async-done | bytes 9830416 | tf_op jit(solution)/shard_map/psum | solution.py:301
  (574 shorter events, 430.1 us)
Async XLA Ops:
  28.1 68.0 %all-gather.7.cloned.1.call-start = ((), (), s32[]{:S(2)}) async-start(), calls=%async_computation.16 | async-start | bytes 1638400 | tf_op jit(solution)/shard_map/all_gather | solution.py:91
  43.2 103.8 %all-reduce.10.cloned.1.call-start = ((), (), s32[]{:S(2)}) async-start(), calls=%async_computation.18 | async-start | bytes 2621440 | tf_op jit(solution)/shard_map/psum | solution.py:121
  108.6 76.3 %all-gather.17.cloned.1.call-start = ((), (), s32[]{:S(2)}) async-start(), calls=%async_computation.22 | async-start | bytes 1638400 | tf_op jit(solution)/shard_map/all_gather | solution.py:90
  152.2 66.3 %all-gather.15.cloned.1.call-start = ((), (), s32[]{:S(2)}) async-start(), calls=%async_computation.21 | async-start | bytes 1638400 | tf_op jit(solution)/shard_map/all_gather | solution.py:91
  155.2 115.7 %all-reduce.12.cloned.1.call-start = ((), (), s32[]{:S(2)}) async-start(), calls=%async_computation.23 | async-start | bytes 2621440 | tf_op jit(solution)/shard_map/psum | solution.py:121
  233.1 94.5 %all-gather.13.cloned.1.call-start = ((), (), s32[]{:S(2)}) async-start(), calls=%async_computation.20 | async-start | bytes 4915200 | tf_op jit(solution)/shard_map/all_gather | solution.py:70
  233.7 173.5 %all-reduce.16.cloned.1.call-start = ((), (), s32[]{:S(2)}) async-start(), calls=%async_computation.41 | async-start | bytes 5242880 | tf_op jit(solution)/shard_map/psum | solution.py:167
  347.1 237.2 %reduce-scatter.37.cloned.1.call-start = ((), (), s32[]{:S(2)}) async-start(), calls=%async_computation.26 | async-start | bytes 1638400 | tf_op jit(solution)/shard_map/reduce_scatter | solution.py:225
  487.2 100.7 %reduce-scatter.39.cloned.1.call-start = ((), (), s32[]{:S(2)}) async-start(), calls=%async_computation.27 | async-start | bytes 1638400 | tf_op jit(solution)/shard_map/reduce_scatter | solution.py:228
  496.0 97.8 %reduce-scatter.33.cloned.1.call-start = ((), (), s32[]{:S(2)}) async-start(), calls=%async_computation.24 | async-start | bytes 1638400 | tf_op jit(solution)/shard_map/reduce_scatter | solution.py:225
  566.3 103.1 %reduce-scatter.63.cloned.1.call-start = ((), (), s32[]{:S(2)}) async-start(), calls=%async_computation.39 | async-start | bytes 1474560
  570.2 101.3 %reduce-scatter.61.cloned.1.call-start = ((), (), s32[]{:S(2)}) async-start(), calls=%async_computation.38 | async-start | bytes 1474560
  575.9 114.6 %reduce-scatter.51.cloned.1.call-start = ((), (), s32[]{:S(2)}) async-start(), calls=%async_computation.33 | async-start | bytes 1474560
  580.9 131.4 %reduce-scatter.49.cloned.1.call-start = ((), (), s32[]{:S(2)}) async-start(), calls=%async_computation.32 | async-start | bytes 1474560
  584.3 149.9 %reduce-scatter.55.cloned.1.call-start = ((), (), s32[]{:S(2)}) async-start(), calls=%async_computation.35 | async-start | bytes 1474560
  587.8 168.3 %reduce-scatter.59.cloned.1.call-start = ((), (), s32[]{:S(2)}) async-start(), calls=%async_computation.37 | async-start | bytes 1474560
  591.2 186.7 %reduce-scatter.53.cloned.1.call-start = ((), (), s32[]{:S(2)}) async-start(), calls=%async_computation.34 | async-start | bytes 1474560
  597.2 202.6 %reduce-scatter.57.cloned.1.call-start = ((), (), s32[]{:S(2)}) async-start(), calls=%async_computation.36 | async-start | bytes 1474560
  629.6 217.8 %reduce-scatter.41.cloned.1.call-start = ((), (), s32[]{:S(2)}) async-start(), calls=%async_computation.28 | async-start | bytes 4915200 | tf_op jit(solution)/shard_map/reduce_scatter | solution.py:293
  635.2 259.9 %reduce-scatter.43.cloned.1.call-start = ((), (), s32[]{:S(2)}) async-start(), calls=%async_computation.29 | async-start | bytes 4915200 | tf_op jit(solution)/shard_map/reduce_scatter | solution.py:293
  640.8 301.5 %reduce-scatter.45.cloned.1.call-start = ((), (), s32[]{:S(2)}) async-start(), calls=%async_computation.30 | async-start | bytes 4915200 | tf_op jit(solution)/shard_map/reduce_scatter | solution.py:296
  646.4 343.1 %reduce-scatter.47.cloned.1.call-start = ((), (), s32[]{:S(2)}) async-start(), calls=%async_computation.31 | async-start | bytes 4915200 | tf_op jit(solution)/shard_map/reduce_scatter | solution.py:296
  651.9 442.6 %all-reduce.14.cloned.1.call-start = ((), (), s32[]{:S(2)}) async-start(), calls=%async_computation.40 | async-start | bytes 10485760 | tf_op jit(solution)/shard_map/psum | solution.py:138
  669.2 771.1 %all-reduce.18.cloned.1.call-start = ((), (), s32[]{:S(2)}) async-start(), calls=%async_computation.42 | async-start | bytes 19660800 | tf_op jit(solution)/shard_map/psum | solution.py:301
  (144 other events, 1071.6 us)
Sparse Core Ops, SparseCore 0:
  28.2 33.9 all-gather.8
  64.3 31.6 all-gather.6
  108.7 38.2 all-reduce.9
  152.4 32.5 all-gather.16
  186.9 31.6 all-gather.14
  232.7 38.2 all-reduce.11
  347.2 59.9 all-reduce.15
  487.3 31.4 reduce-scatter.36
  521.7 30.0 reduce-scatter.38
  562.6 31.2 reduce-scatter.32
  596.2 30.0 reduce-scatter.34
  649.0 19.6 reduce-scatter.60
  670.8 19.6 reduce-scatter.50
  692.6 19.6 reduce-scatter.48
  714.5 19.6 reduce-scatter.54
  736.3 19.6 reduce-scatter.58
  758.1 19.6 reduce-scatter.52
  780.1 19.6 reduce-scatter.56
  802.5 44.8 reduce-scatter.40
  850.2 44.8 reduce-scatter.42
  897.4 44.8 reduce-scatter.44
  944.6 44.8 reduce-scatter.46
  991.9 102.5 all-reduce.13
  1099.9 340.3 all-reduce.17
  (1 shorter events, 18.3 us)
Sparse Core Ops, SparseCore 1:
  234.6 45.3 all-gather.10
  281.4 46.2 all-gather.12
where the time goes:
time: 1470 us; the launch traced here: 1460 us
  waiting for transfers between devices  959 us (65%)
  matrix products  225 us (15%)
  local copies, waits for them, and re-layouts  97 us (7%)
  blocking collectives  86.5 us (6%)
  other arithmetic  63.9 us (4%)
  between operations  18.4 us (1%)
    psum x1, waiting for transfers between devices, per_device(): lax.psum(scattered[0].astype(jnp.bfloat16), 'ctx').astype(jnp.float32)  285 us
    unnamed x35, waiting for transfers between devices  118 us
    psum x1, waiting for transfers between devices, per_device(): lax.psum(partial_ffn.astype(jnp.bfloat16), 'tp').astype(jnp.float32)  104 us
    reduce_scatter x2, waiting for transfers between devices, per_device(): lax.psum_scatter(local_grads[5].astype(jnp.bfloat16), 'shard', scatter_di...  94.3 us
    reduce_scatter x2, waiting for transfers between devices, per_device(): lax.psum_scatter(local_grads[4].astype(jnp.bfloat16), 'shard', scatter_di...  93.3 us
    psum x2, waiting for transfers between devices, per_device(): lax.psum(partial_out.astype(jnp.bfloat16), 'tp').astype(jnp.float32)  73.4 us
    psum x1, waiting for transfers between devices, per_device(): lax.psum(partial_two.astype(jnp.bfloat16), 'tp').astype(jnp.float32)  60 us
    unnamed x238, local copies, waits for them, and re-layouts  51.3 us
  transfers between devices with their start and end apart: 27, of which 22 were waited for; matrix products, arithmetic and copies ran while one was open for 16% of the time, Pallas kernels for 0%

commit v1 on v0

--- a/solution.py
+++ b/solution.py
@@ -87,8 +87,13 @@
         ).astype(half_kind)
         query_heads = queries.reshape(frame_rows, head_count, HD)
         start = jnp.int32(0)
-        key_piece = lax.all_gather(key_rows, "ctx", axis=0, tiled=True)
-        value_piece = lax.all_gather(value_rows, "ctx", axis=0, tiled=True)
+        key_piece, value_piece = jnp.split(
+            lax.all_gather(
+                jnp.concatenate([key_rows, value_rows], axis=1), "ctx", axis=0, tiled=True
+            ),
+            [key_rows.shape[1]],
+            axis=1,
+        )
         unnormal = jnp.zeros((frame_rows, head_count, HD), float_kind)
         weight_total = jnp.zeros((frame_rows, head_count), float_kind)
         piece_rows = key_piece.shape[0]

time: 1470 us -> 1520 us (1.034)
  waiting for transfers between devices: 959 us -> 1030 us
    all_gather x4 -> x6, waiting for transfers between devices: 66.6 us -> 135 us  [the longest x2 80.8 us: per_device(): lax.all_gather(jnp.concatenate([key_rows, value_rows], axis=1), 'ctx', ax...]
    unnamed x238 -> x230, local copies, waits for them, and re-layouts: 51.3 us -> 47.8 us
    unnamed x35 -> x37, waiting for transfers between devices: 118 us -> 121 us
  transfers between devices with their start and end apart: 27 -> 29, of which waited for: 22 -> 23; matrix products, arithmetic and copies ran while one was open for 16% -> 18% of each run, Pallas kernels for 0% -> 0%
where the time goes in v1:
time: 1520 us; the launch traced here: 1510 us
  waiting for transfers between devices  1030 us (68%)
  matrix products  211 us (14%)
  local copies, waits for them, and re-layouts  90.8 us (6%)
  blocking collectives  86.5 us (6%)
  other arithmetic  67.2 us (4%)
  between operations  18.6 us (1%)
    psum x1, waiting for transfers between devices, per_device(): lax.psum(scattered[0].astype(jnp.bfloat16), 'ctx').astype(jnp.float32)  285 us
    unnamed x37, waiting for transfers between devices  121 us
    psum x1, waiting for transfers between devices, per_device(): lax.psum(partial_ffn.astype(jnp.bfloat16), 'tp').astype(jnp.float32)  104 us
    reduce_scatter x2, waiting for transfers between devices, per_device(): lax.psum_scatter(local_grads[5].astype(jnp.bfloat16), 'shard', scatter_di...  94.1 us
    reduce_scatter x2, waiting for transfers between devices, per_device(): lax.psum_scatter(local_grads[4].astype(jnp.bfloat16), 'shard', scatter_di...  93.5 us
    all_gather x2, waiting for transfers between devices, per_device(): lax.all_gather(jnp.concatenate([key_rows, value_rows], axis=1), 'ctx', ax...  80.8 us
    psum x2, waiting for transfers between devices, per_device(): lax.psum(partial_out.astype(jnp.bfloat16), 'tp').astype(jnp.float32)  72.8 us
    psum x1, waiting for transfers between devices, per_device(): lax.psum(partial_two.astype(jnp.bfloat16), 'tp').astype(jnp.float32)  57.2 us
  transfers between devices with their start and end apart: 29, of which 23 were waited for; matrix products, arithmetic and copies ran while one was open for 18% of the time, Pallas kernels for 0%

profile of v1, /device:TPU:0, one launch (start us, length us, event | category | flops | bytes accessed | tf_op | source)
XLA Modules:
  0.0 1507.2 jit_solution(17208730551355677040)
XLA Ops:
  69.5 30.4 %all-gather.9.cloned.1.call-done = bf16[2048,640]{0,1:T(8,128)(2,1)} async-done(((bf16[512,640]{0,1:T(8,128)(2,1)}), bf16[2048,640]{0,1:T(8,128)(2,1)}) %all-gather.9.cloned.1.call-update) | async-done | bytes 2621456 | tf_op jit(solution)/shard_map/all_gather | solution.py:91
  113.7 37.5 %all-reduce.10.cloned.1.call-done = bf16[512,1280]{1,0:T(8,128)(2,1)} async-done(((bf16[512,1280]{1,0:T(8,128)(2,1)}), bf16[512,1280]{1,0:T(8,128)(2,1)}) %all-reduce.10.cloned.1.call-update) | async-done | bytes 1310736 | tf_op jit(solution)/shard_map/psum | solution.py:126
  165.6 50.4 %all-gather.15.cloned.1.call-done = bf16[2048,640]{0,1:T(8,128)(2,1)} async-done(((bf16[512,640]{0,1:T(8,128)(2,1)}), bf16[2048,640]{0,1:T(8,128)(2,1)}) %all-gather.15.cloned.1.call-update) | async-done | bytes 2621456 | tf_op jit(solution)/shard_map/all_gather | solution.py:91
  232.0 35.3 %all-reduce.12.cloned.1.call-done = bf16[512,1280]{1,0:T(8,128)(2,1)} async-done(((bf16[512,1280]{1,0:T(8,128)(2,1)}), bf16[512,1280]{1,0:T(8,128)(2,1)}) %all-reduce.12.cloned.1.call-update) | async-done | bytes 1310736 | tf_op jit(solution)/shard_map/psum | solution.py:126
  297.6 26.4 %all-gather.13.cloned.1.call-done = bf16[1280,1280]{1,0:T(8,128)(2,1)} async-done(((bf16[640,1280]{1,0:T(8,128)(2,1)}), bf16[1280,1280]{1,0:T(8,128)(2,1)}) %all-gather.13.cloned.1.call-update) | async-done | bytes 3276816 | tf_op jit(solution)/shard_map/all_gather | solution.py:70
  346.3 57.2 %all-reduce.16.cloned.1.call-done = (bf16[512,1280]{1,0:T(8,128)(2,1)}, bf16[512,1280]{1,0:T(8,128)(2,1)}) async-done(((bf16[512,1280]{1,0:T(8,128)(2,1)}, bf16[512,1280]{1,0:T(8,128)(2,1)}), (bf16[512,1280]{1,0:T(8,128)(2,1)}, bf16[512,1280]{1,0:T(8,128)(2,1)})) %all-reduce.16.cloned.1.call-update) | async-done | bytes 2621456 | tf_op jit(solution)/shard_map/psum | solution.py:172
  417.2 20.5 %all-gather.21.cloned.1.call-done = bf16[2048,320]{0,1:T(8,128)(2,1)} async-done(((bf16[512,320]{0,1:T(8,128)(2,1)}), bf16[2048,320]{0,1:T(8,128)(2,1)}) %all-gather.21.cloned.1.call-update) | async-done | bytes 1310736 | tf_op jit(solution)/shard_map/all_gather | solution.py:184
  437.6 33.2 %all-gather.23.cloned.1.call-done = bf16[2048,320]{0,1:T(8,128)(2,1)} async-done(((bf16[512,320]{0,1:T(8,128)(2,1)}), bf16[2048,320]{0,1:T(8,128)(2,1)}) %all-gather.23.cloned.1.call-update) | async-done | bytes 1310736 | tf_op jit(solution)/shard_map/all_gather | solution.py:185
  473.2 59.8 %while.31 = (s32[]{:T(128)}, f32[512,4,80]{0,2,1:T(8,128)}, bf16[4,512,4,80]{1,3,2,0:T(8,128)(2,1)}, bf16[4,512,4,80]{1,3,2,0:T(8,128)(2,1)}, s32[4]{0:T(128)S(1...) while((s32[]{:T(128)}, f32[512,4,80]{0,2,1:T(8,128)}, ...), condition=%wide.region_36.37_spmd.clone, body=%wide.region_35.36_spmd.clone.sunk | while | flops 848626688 | bytes 52898636 | solution.py:222
  548.3 60.3 %while.30 = (s32[]{:T(128)}, f32[512,4,80]{0,2,1:T(8,128)}, bf16[4,512,4,80]{1,3,2,0:T(8,128)(2,1)}, bf16[4,512,4,80]{1,3,2,0:T(8,128)(2,1)}, s32[4]{0:T(128)S(1...) while((s32[]{:T(128)}, f32[512,4,80]{0,2,1:T(8,128)}, ...), condition=%wide.region_25.26_spmd.clone, body=%wide.region_24.25_spmd.clone.sunk | while | flops 848626688 | bytes 52898636 | solution.py:222
  646.4 29.0 %reduce-scatter.35.cloned.1.call-done = bf16[512,320]{0,1:T(8,128)(2,1)} async-done(((bf16[2048,320]{0,1:T(8,128)(2,1)}), bf16[512,320]{0,1:T(8,128)(2,1)}) %reduce-scatter.35.cloned.1.call-update) | async-done | bytes 327696 | tf_op jit(solution)/shard_map/reduce_scatter | solution.py:233
  722.7 16.9 %reduce-scatter.51.cloned.1.call-done = bf16[640,320]{1,0:T(8,128)(2,1)} async-done(((bf16[1280,320]{1,0:T(8,128)(2,1)}), bf16[640,320]{1,0:T(8,128)(2,1)}) %reduce-scatter.51.cloned.1.call-update) | async-done | bytes 409616
  741.5 19.9 %reduce-scatter.49.cloned.1.call-done = bf16[640,320]{1,0:T(8,128)(2,1)} async-done(((bf16[1280,320]{1,0:T(8,128)(2,1)}), bf16[640,320]{1,0:T(8,128)(2,1)}) %reduce-scatter.49.cloned.1.call-update) | async-done | bytes 409616
  763.4 19.9 %reduce-scatter.55.cloned.1.call-done = bf16[640,320]{1,0:T(8,128)(2,1)} async-done(((bf16[1280,320]{1,0:T(8,128)(2,1)}), bf16[640,320]{1,0:T(8,128)(2,1)}) %reduce-scatter.55.cloned.1.call-update) | async-done | bytes 409616
  785.2 20.0 %reduce-scatter.59.cloned.1.call-done = bf16[640,320]{1,0:T(8,128)(2,1)} async-done(((bf16[1280,320]{1,0:T(8,128)(2,1)}), bf16[640,320]{1,0:T(8,128)(2,1)}) %reduce-scatter.59.cloned.1.call-update) | async-done | bytes 409616
  807.2 19.9 %reduce-scatter.53.cloned.1.call-done = bf16[640,320]{1,0:T(8,128)(2,1)} async-done(((bf16[1280,320]{1,0:T(8,128)(2,1)}), bf16[640,320]{1,0:T(8,128)(2,1)}) %reduce-scatter.53.cloned.1.call-update) | async-done | bytes 409616
  829.0 20.0 %reduce-scatter.57.cloned.1.call-done = bf16[640,320]{1,0:T(8,128)(2,1)} async-done(((bf16[1280,320]{1,0:T(8,128)(2,1)}), bf16[640,320]{1,0:T(8,128)(2,1)}) %reduce-scatter.57.cloned.1.call-update) | async-done | bytes 409616
  851.0 45.8 %reduce-scatter.41.cloned.1.call-done = bf16[640,1280]{1,0:T(8,128)(2,1)} async-done(((bf16[1280,1280]{1,0:T(8,128)(2,1)}), bf16[640,1280]{1,0:T(8,128)(2,1)}) %reduce-scatter.41.cloned.1.call-update) | async-done | bytes 1638416 | tf_op jit(solution)/shard_map/reduce_scatter | solution.py:298
  896.7 47.7 %reduce-scatter.43.cloned.1.call-done = bf16[640,1280]{1,0:T(8,128)(2,1)} async-done(((bf16[1280,1280]{1,0:T(8,128)(2,1)}), bf16[640,1280]{1,0:T(8,128)(2,1)}) %reduce-scatter.43.cloned.1.call-update) | async-done | bytes 1638416 | tf_op jit(solution)/shard_map/reduce_scatter | solution.py:298
  944.5 47.0 %reduce-scatter.45.cloned.1.call-done = bf16[640,1280]{1,0:T(8,128)(2,1)} async-done(((bf16[1280,1280]{1,0:T(8,128)(2,1)}), bf16[640,1280]{1,0:T(8,128)(2,1)}) %reduce-scatter.45.cloned.1.call-update) | async-done | bytes 1638416 | tf_op jit(solution)/shard_map/reduce_scatter | solution.py:301
  991.5 47.1 %reduce-scatter.47.cloned.1.call-done = bf16[640,1280]{1,0:T(8,128)(2,1)} async-done(((bf16[1280,1280]{1,0:T(8,128)(2,1)}), bf16[640,1280]{1,0:T(8,128)(2,1)}) %reduce-scatter.47.cloned.1.call-update) | async-done | bytes 1638416 | tf_op jit(solution)/shard_map/reduce_scatter | solution.py:301
  1039.8 103.9 %all-reduce.14.cloned.1.call-done = (bf16[512,1280]{1,0:T(8,128)(2,1)}, bf16[512,1280]{1,0:T(8,128)(2,1)}, bf16[512,1280]{1,0:T(8,128)(2,1)}, bf16[512,1280]{1,0:T(8,128)(2,1)}) async-done(((bf16[512,1280]{1,0:T(8,128)(2,1)}, bf16[512,1280]{1,0:T(8,128)(2,1)}, bf16[512,1280]{1,0:T(8,128)(2,1)}, bf16[512,1280]{1,0:T(8,128)(2,1)}), (bf16[512,1280]{1,0:T(8,128)(2,1)}, bf16[512,1280]{1,0:T(8,128)(2,1)}, ...) | async-done | bytes 5242896 | tf_op jit(solution)/shard_map/psum | solution.py:143
  1153.6 41.8 %all-reduce = (f32[1280]{0:T(1024)}, f32[1280]{0:T(1024)}, f32[320]{0:T(512)}, f32[320]{0:T(512)}, f32[1280]{0:T(1024)}, /*index=5*/f32[1280]{0:T(1024)}, f32[1280]{0:T(1024)}, f32[1280]{0:T(1024)}, f32[1280]{0:T(1024)}) all-reduce(f32[1280]{0:T(1024)S(1)} %add.526, ...), channel_id=1, replica_groups=mesh['shard'=2,'ctx'=4,'tp'=4] {'shard','ctx'}, use_global_device_ids=true, to_apply=%region_44.45 | all-reduce | flops 9600 | bytes 76800 | tf_op jit(solution)/shard_map/psum | solution.py:318
  1204.2 285.2 %all-reduce.18.cloned.1.call-done = (bf16[640,320]{0,1:T(8,128)(2,1)}, bf16[640,320]{0,1:T(8,128)(2,1)}, bf16[640,320]{0,1:T(8,128)(2,1)}, bf16[640,320]{0,1:T(8...) async-done(((bf16[640,320]{0,1:T(8,128)(2,1)}, ...) | async-done | bytes 9830416 | tf_op jit(solution)/shard_map/psum | solution.py:306
  (572 shorter events, 428.0 us)
Async XLA Ops:
  43.8 107.4 %all-reduce.10.cloned.1.call-start = ((), (), s32[]{:S(2)}) async-start(), calls=%async_computation.17 | async-start | bytes 2621440 | tf_op jit(solution)/shard_map/psum | solution.py:126
  113.1 102.9 %all-gather.15.cloned.1.call-start = ((), (), s32[]{:S(2)}) async-start(), calls=%async_computation.20 | async-start | bytes 3276800 | tf_op jit(solution)/shard_map/all_gather | solution.py:91
  161.1 106.2 %all-reduce.12.cloned.1.call-start = ((), (), s32[]{:S(2)}) async-start(), calls=%async_computation.21 | async-start | bytes 2621440 | tf_op jit(solution)/shard_map/psum | solution.py:126
  230.4 173.2 %all-reduce.16.cloned.1.call-start = ((), (), s32[]{:S(2)}) async-start(), calls=%async_computation.43 | async-start | bytes 5242880 | tf_op jit(solution)/shard_map/psum | solution.py:172
  344.0 126.8 %all-gather.23.cloned.1.call-start = ((), (), s32[]{:S(2)}) async-start(), calls=%async_computation.27 | async-start | bytes 1638400 | tf_op jit(solution)/shard_map/all_gather | solution.py:185
  344.8 201.0 %all-gather.19.cloned.1.call-start = ((), (), s32[]{:S(2)}) async-start(), calls=%async_computation.23 | async-start | bytes 1638400 | tf_op jit(solution)/shard_map/all_gather | solution.py:185
  345.5 200.2 %all-gather.17.cloned.1.call-start = ((), (), s32[]{:S(2)}) async-start(), calls=%async_computation.22 | async-start | bytes 1638400 | tf_op jit(solution)/shard_map/all_gather | solution.py:184
  346.3 288.0 %reduce-scatter.37.cloned.1.call-start = ((), (), s32[]{:S(2)}) async-start(), calls=%async_computation.28 | async-start | bytes 1638400 | tf_op jit(solution)/shard_map/reduce_scatter | solution.py:230
  536.9 100.9 %reduce-scatter.39.cloned.1.call-start = ((), (), s32[]{:S(2)}) async-start(), calls=%async_computation.29 | async-start | bytes 1638400 | tf_op jit(solution)/shard_map/reduce_scatter | solution.py:233
  545.7 97.3 %reduce-scatter.33.cloned.1.call-start = ((), (), s32[]{:S(2)}) async-start(), calls=%async_computation.24 | async-start | bytes 1638400 | tf_op jit(solution)/shard_map/reduce_scatter | solution.py:230
  616.2 102.5 %reduce-scatter.63.cloned.1.call-start = ((), (), s32[]{:S(2)}) async-start(), calls=%async_computation.41 | async-start | bytes 1474560
  620.3 100.5 %reduce-scatter.61.cloned.1.call-start = ((), (), s32[]{:S(2)}) async-start(), calls=%async_computation.40 | async-start | bytes 1474560
  626.0 113.6 %reduce-scatter.51.cloned.1.call-start = ((), (), s32[]{:S(2)}) async-start(), calls=%async_computation.35 | async-start | bytes 1474560
  630.9 130.4 %reduce-scatter.49.cloned.1.call-start = ((), (), s32[]{:S(2)}) async-start(), calls=%async_computation.34 | async-start | bytes 1474560
  634.2 149.0 %reduce-scatter.55.cloned.1.call-start = ((), (), s32[]{:S(2)}) async-start(), calls=%async_computation.37 | async-start | bytes 1474560
  637.7 167.5 %reduce-scatter.59.cloned.1.call-start = ((), (), s32[]{:S(2)}) async-start(), calls=%async_computation.39 | async-start | bytes 1474560
  641.1 185.9 %reduce-scatter.53.cloned.1.call-start = ((), (), s32[]{:S(2)}) async-start(), calls=%async_computation.36 | async-start | bytes 1474560
  646.4 202.6 %reduce-scatter.57.cloned.1.call-start = ((), (), s32[]{:S(2)}) async-start(), calls=%async_computation.38 | async-start | bytes 1474560
  678.8 217.9 %reduce-scatter.41.cloned.1.call-start = ((), (), s32[]{:S(2)}) async-start(), calls=%async_computation.30 | async-start | bytes 4915200 | tf_op jit(solution)/shard_map/reduce_scatter | solution.py:298
  684.4 260.1 %reduce-scatter.43.cloned.1.call-start = ((), (), s32[]{:S(2)}) async-start(), calls=%async_computation.31 | async-start | bytes 4915200 | tf_op jit(solution)/shard_map/reduce_scatter | solution.py:298
  690.0 301.5 %reduce-scatter.45.cloned.1.call-start = ((), (), s32[]{:S(2)}) async-start(), calls=%async_computation.32 | async-start | bytes 4915200 | tf_op jit(solution)/shard_map/reduce_scatter | solution.py:301
  695.5 343.1 %reduce-scatter.47.cloned.1.call-start = ((), (), s32[]{:S(2)}) async-start(), calls=%async_computation.33 | async-start | bytes 4915200 | tf_op jit(solution)/shard_map/reduce_scatter | solution.py:301
  701.1 442.6 %all-reduce.14.cloned.1.call-start = ((), (), s32[]{:S(2)}) async-start(), calls=%async_computation.42 | async-start | bytes 10485760 | tf_op jit(solution)/shard_map/psum | solution.py:143
  718.5 770.9 %all-reduce.18.cloned.1.call-start = ((), (), s32[]{:S(2)}) async-start(), calls=%async_computation.44 | async-start | bytes 19660800 | tf_op jit(solution)/shard_map/psum | solution.py:306
  (142 other events, 1314.0 us)
Sparse Core Ops, SparseCore 0:
  43.9 55.9 all-gather.8
  113.2 37.8 all-reduce.9
  161.2 54.7 all-gather.14
  229.4 37.8 all-reduce.11
  343.6 59.9 all-reduce.15
  405.0 32.5 all-gather.20
  439.2 31.6 all-gather.22
  472.4 31.6 all-gather.18
  505.6 31.5 all-gather.16
  539.4 30.5 reduce-scatter.36
  572.9 30.0 reduce-scatter.38
  612.5 30.5 reduce-scatter.32
  645.3 30.0 reduce-scatter.34
  698.0 19.6 reduce-scatter.60
  719.8 19.6 reduce-scatter.50
  741.7 19.6 reduce-scatter.48
  763.5 19.6 reduce-scatter.54
  807.3 19.6 reduce-scatter.52
  851.8 44.8 reduce-scatter.40
  899.6 44.8 reduce-scatter.42
  946.6 44.8 reduce-scatter.44
  993.7 44.8 reduce-scatter.46
  1041.0 102.5 all-reduce.13
  1148.9 340.4 all-reduce.17
  (3 shorter events, 57.5 us)
Sparse Core Ops, SparseCore 1:
  231.3 45.0 all-gather.10
  277.7 46.2 all-gather.12
